TPU v7x, 32 devices: a whole 2x2x4 slice. The times are simulated.
32 devices in a mesh: sens: 2 (over x), sx: 4 (over z), sy: 4 (over y, core).
Axes of the slice: x: 2, y: 2, z: 4, core: 2. Of those that a mesh axis runs over, the one named last changes fastest.
Arguments:
- records: bfloat16 [4, 128, 128], P(None, 'sens'), may hold values from -6 to 6
- kernel: bfloat16 [128, 64, 32, 128], P('sens', 'sx', 'sy'), may hold values from -0.09375 to 0.09375
- diffusion: float32 [64, 32], P('sx', 'sy'), may hold values from 0.04 to 0.24
Outputs:
- predicted: float32 [4, 128, 128], P(None, ('sens', 'sx', 'sy'))
All inputs are finite; a program needn't handle non-finite values.
Results may differ from a plain program's by a relative error of at most 0.0011.
Values may be sent and summed in bfloat16 or wider, within the bound.
A program may use at most 64 MiB of HBM per device.

v0:
```python
import jax
import jax.numpy as jnp
from jax import lax
from jax.sharding import PartitionSpec as P

SWEEPS = 4


def extended(shard, sides, width):
    for axis, dim in sides:
        count, length = (lax.axis_size(axis), shard.shape[dim])
        up = [(i, (i + 1) % count) for i in range(count - 1)]
        down = [(j, i) for i, j in up]
        last = lax.slice_in_dim(shard, length - width, length, axis=dim)
        first = lax.slice_in_dim(shard, 0, width, axis=dim)
        before = lax.ppermute(last, axis, up)
        after = lax.ppermute(first, axis, down)
        shard = jnp.concatenate([before, shard, after], axis=dim)
    return shard


def neighbours(padded):
    return padded[:, 2:, 1:-1] + padded[:, :-2, 1:-1] + padded[:, 1:-1, 2:] + padded[:, 1:-1, :-2]


def smooth(prior_field, diffusion):
    weights = diffusion[None, :, :, None]
    margin = SWEEPS
    padded, rate_wide = (
        extended(prior_field, (("sx", 1), ("sy", 2)), margin),
        extended(weights, (("sx", 1), ("sy", 2)), margin),
    )
    for repeat in range(margin):
        interior = padded[:, 1:-1, 1:-1]
        rate_wide = rate_wide[:, 1:-1, 1:-1]
        padded = interior + rate_wide * (neighbours(padded) - 4.0 * interior)
    return padded


def per_device(records, kernel, diffusion):
    vectors, sensors, window = records.shape
    cells_x, cells_y = diffusion.shape
    kernel_rows = kernel.reshape(kernel.shape[0], cells_x * cells_y, window)
    partials = lax.conv_general_dilated(
        records,
        kernel_rows,
        (1,),
        [(0, window - 1)],
        dimension_numbers=("NCH", "IOH", "NCH"),
        preferred_element_type=jnp.float32,
    )
    partials = partials.reshape(vectors, cells_x, cells_y, window)
    whole_sum = lax.psum(partials, "sens")
    smoothed = smooth(whole_sum, diffusion).astype(jnp.bfloat16)
    flipped = smoothed.reshape(vectors, cells_x * cells_y, window)[:, :, ::-1]
    backward = lax.conv_general_dilated(
        flipped,
        kernel_rows,
        (1,),
        [(0, window - 1)],
        dimension_numbers=("NCH", "OIH", "NCH"),
        preferred_element_type=jnp.float32,
    )
    summands = backward[:, :, ::-1]
    return lax.psum_scatter(summands, ("sx", "sy"), scatter_dimension=1, tiled=True)


def solution(mesh):
    return jax.shard_map(
        per_device,
        mesh=mesh,
        in_specs=(P(None, "sens", None), P("sens", "sx", "sy", None), P("sx", "sy")),
        out_specs=P(None, ("sens", "sx", "sy"), None),
        check_vma=False,
    )
```

profile of v0, /device:TPU:8, one launch (start us, length us, event | category | flops | bytes accessed | tf_op | source)
XLA Modules:
  0.0 175.8 jit_solution(15188670381473331746)
XLA Ops:
  6.5 0.0 all-reduce.4.cloned.1.call-start
  6.5 0.8 fusion.17
  7.4 1.9 %collective-permute-start.5 = (f32[1,4,8,1]{1,2,3,0:T(8,128)S(1)}, f32[1,4,8,1]{1,2,3,0:T(8,128)S(1)}, u32[]{:S(2)}, u32[]{:S(2)}) collective-permute-start(f32[1,4,8,1]{1,2,3,0:T(8,128)S(1)} %get-tuple-element.12), channel_id=1, source_target_pairs={{4,0},{8,4},{12,8},{5,1},{9,5},{13,9},{6,2},{10,6},{14,10},{7,3},{... | collective-permute-start | bytes 392 | tf_op jit(solution)/shard_map/ppermute | solution.py:17
  9.3 3.9 %collective-permute-start.4 = (f32[1,4,8,1]{1,2,3,0:T(8,128)S(1)}, f32[1,4,8,1]{1,2,3,0:T(8,128)S(1)}, u32[]{:S(2)}, u32[]{:S(2)}) collective-permute-start(f32[1,4,8,1]{1,2,3,0:T(8,128)S(1)} %get-tuple-element.11), channel_id=1, source_target_pairs={{0,4},{4,8},{8,12},{1,5},{5,9},{9,13},{2,6},{6,10},{10,14},{3,7},{... | collective-permute-start | bytes 392 | tf_op jit(solution)/shard_map/ppermute | solution.py:16
  13.2 1.0 copy.22
  14.2 0.0 copy-start
  14.2 3.3 %copy.23 = bf16[64,128,128]{1,0,2:T(8,128)(2,1)S(1)} copy(bf16[64,128,128]{2,1,0:T(8,128)(2,1)} %bitcast.16) | data formatting | bytes 4194304 | tf_op jit(solution)/shard_map/reshape | solution.py:43
  17.5 0.0 collective-permute-done.5
  17.5 0.0 collective-permute-done.4
  17.5 0.0 copy-done
  17.5 0.1 pad_maximum_fusion.2
  17.6 1.3 collective-permute-start.7
  18.9 3.0 %collective-permute-start.6 = (f32[1,24,4,1]{1,2,3,0:T(4,128)S(1)}, f32[1,24,4,1]{1,2,3,0:T(4,128)S(1)}, u32[]{:S(2)}, u32[]{:S(2)}) collective-permute-start(f32[1,24,4,1]{1,2,3,0:T(4,128)S(1)} %get-tuple-element.9), channel_id=1, source_target_pairs={{0,1},{1,2},{2,3},{4,5},{5,6},{6,7},{8,9},{9,10},{10,11},{12,13},{... | collective-permute-start | bytes 1160 | tf_op jit(solution)/shard_map/ppermute | solution.py:16
  22.0 2.9 %fusion.18 = f32[4,128,128]{1,0,2:T(4,128)S(1)} fusion(bf16[4,64,128]{1,0,2:T(4,128)(2,1)S(1)} %copy.22, bf16[64,128,128]{1,0,2:T(8,128)(2,1)S(1)} %copy.23), kind=kOutput, calls=%fused_computation.40 | convolution fusion | flops 541065216 | bytes 2424832 | tf_op jit(solution)/shard_map/conv_general_dilated | solution.py:44
  24.9 0.8 copy.24
  25.7 0.0 all-reduce.4.cloned.1.call-update
  25.8 0.0 all-reduce.6.cloned.1.call-start
  25.8 0.1 copy.28
  25.9 0.0 collective-permute-done.7
  25.9 0.0 collective-permute-done.6
  25.9 0.1 pad_maximum_fusion.1
  26.0 0.1 slice_bitcast_fusion.2
  26.1 23.3 %all-reduce.4.cloned.1.call-done = f32[4,16,8,128]{3,2,1,0:T(8,128)} async-done(((f32[4,16,8,128]{3,2,1,0:T(8,128)}), f32[4,16,8,128]{3,2,1,0:T(8,128)}) %all-reduce.4.cloned.1.call-update) | async-done | bytes 262160 | tf_op jit(solution)/shard_map/psum | solution.py:53
  49.4 0.9 fusion.15
  50.3 3.4 %collective-permute-start = (f32[4,4,8,128]{3,2,1,0:T(8,128)S(1)}, f32[4,4,8,128]{3,2,1,0:T(8,128)S(1)}, u32[]{:S(2)}, u32[]{:S(2)}) collective-permute-start(f32[4,4,8,128]{3,2,1,0:T(8,128)S(1)} %get-tuple-element.8), channel_id=1, source_target_pairs={{0,4},{4,8},{8,12},{1,5},{5,9},{9,13},{2,6},{6,10},{10,14},{3,7},{... | collective-permute-start | bytes 196616 | tf_op jit(solution)/shard_map/ppermute | solution.py:16
  53.7 0.1 slice_bitcast_fusion.1
  53.7 0.1 copy.25
  53.8 0.1 copy.26
  53.9 2.4 %collective-permute-start.1 = (f32[4,4,8,128]{3,2,1,0:T(8,128)S(1)}, f32[4,4,8,128]{3,2,1,0:T(8,128)S(1)}, u32[]{:S(2)}, u32[]{:S(2)}) collective-permute-start(f32[4,4,8,128]{3,2,1,0:T(8,128)S(1)} %get-tuple-element.7), channel_id=1, source_target_pairs={{4,0},{8,4},{12,8},{5,1},{9,5},{13,9},{6,2},{10,6},{14,10},{7,3},{... | collective-permute-start | bytes 196616 | tf_op jit(solution)/shard_map/ppermute | solution.py:17
  56.4 0.0 collective-permute-done
  56.4 1.0 constant_dynamic-update-slice_fusion.1
  57.4 2.7 %collective-permute-done.1 = f32[4,4,8,128]{3,2,1,0:T(8,128)S(1)} collective-permute-done((f32[4,4,8,128]{3,2,1,0:T(8,128)S(1)}, f32[4,4,8,128]{3,2,1,0:T(8,128)S(1)}, u32[]{:S(2)}, u32[]{:S(2)}) %collective-permute-start.1) | collective-permute-done | bytes 65568 | tf_op jit(solution)/shard_map/ppermute | solution.py:17
  60.1 0.1 fusion.14
  60.1 1.3 collective-permute-start.3
  61.4 3.0 %collective-permute-start.2 = (f32[4,24,4,128]{3,2,1,0:T(4,128)S(1)}, f32[4,24,4,128]{3,2,1,0:T(4,128)S(1)}, u32[]{:S(2)}, u32[]{:S(2)}) collective-permute-start(f32[4,24,4,128]{3,2,1,0:T(4,128)S(1)} %get-tuple-element.5), channel_id=1, source_target_pairs={{0,1},{1,2},{2,3},{4,5},{5,6},{6,7},{8,9},{9,10},{10,11},{12,13},{... | collective-permute-start | bytes 589832 | tf_op jit(solution)/shard_map/ppermute | solution.py:16
  64.5 0.1 slice_bitcast_fusion
  64.6 0.1 copy.27
  64.7 0.0 collective-permute-done.3
  64.7 0.9 collective-permute-done.2
  65.5 0.2 pad_maximum_fusion
  65.7 0.3 fusion.2
  66.0 0.2 fusion.5
  66.2 0.2 fusion.8
  66.5 0.1 fusion.13
  66.6 0.0 copy-start.1
  66.6 0.4 rev.6
  67.0 0.1 copy.29
  67.2 6.1 %fusion.19 = f32[4,64,128]{1,0,2:T(4,128)S(1)} fusion(bf16[4,128,128]{1,0,2:T(4,128)(2,1)S(1)} %copy.29, bf16[64,128,128]{1,0,2:T(8,128)(2,1)S(1)} %copy.23), kind=kOutput, calls=%fused_computation.41 | convolution fusion | flops 541065216 | bytes 2359296 | tf_op jit(solution)/shard_map/conv_general_dilated | solution.py:56
  73.3 0.8 copy.31
  74.1 0.0 all-reduce.6.cloned.1.call-update
  74.1 0.0 copy-done.1
  74.2 0.6 dynamic-slice
  75.4 92.2 %all-reduce.6.cloned.1.call-done = f32[4,64,128]{2,0,1:T(4,128)} async-done(((f32[4,64,128]{2,0,1:T(4,128)}), f32[4,64,128]{2,0,1:T(4,128)}) %all-reduce.6.cloned.1.call-update) | async-done | bytes 131088
  167.6 0.7 constant_dynamic-slice_fusion
  168.3 0.6 copy.32
  (4 shorter events, 0.1 us)
Async XLA Ops:
  6.5 42.8 %all-reduce.4.cloned.1.call-start = ((), (), s32[]{:S(2)}) async-start(), calls=%async_computation | async-start | bytes 524288 | tf_op jit(solution)/shard_map/psum | solution.py:53
  7.4 10.1 %collective-permute-start.5 = (f32[1,4,8,1]{1,2,3,0:T(8,128)S(1)}, f32[1,4,8,1]{1,2,3,0:T(8,128)S(1)}, u32[]{:S(2)}, u32[]{:S(2)}) collective-permute-start(f32[1,4,8,1]{1,2,3,0:T(8,128)S(1)} %get-tuple-element.12), channel_id=1, source_target_pairs={{4,0},{8,4},{12,8},{5,1},{9,5},{13,9},{6,2},{10,6},{14,10},{7,3},{... | collective-permute-start | bytes 392 | tf_op jit(solution)/shard_map/ppermute | solution.py:17
  9.3 8.2 %collective-permute-start.4 = (f32[1,4,8,1]{1,2,3,0:T(8,128)S(1)}, f32[1,4,8,1]{1,2,3,0:T(8,128)S(1)}, u32[]{:S(2)}, u32[]{:S(2)}) collective-permute-start(f32[1,4,8,1]{1,2,3,0:T(8,128)S(1)} %get-tuple-element.11), channel_id=1, source_target_pairs={{0,4},{4,8},{8,12},{1,5},{5,9},{9,13},{2,6},{6,10},{10,14},{3,7},{... | collective-permute-start | bytes 392 | tf_op jit(solution)/shard_map/ppermute | solution.py:16
  14.2 3.3 %copy-start = (f32[16,8]{0,1:T(8,128)S(1)}, f32[16,8]{0,1:T(8,128)}, u32[]{:S(2)}) copy-start(f32[16,8]{0,1:T(8,128)} %param.5) | copy-start | bytes 1540
  17.6 8.3 %collective-permute-start.7 = (f32[1,24,4,1]{1,2,3,0:T(4,128)S(1)}, f32[1,24,4,1]{1,2,3,0:T(4,128)S(1)}, u32[]{:S(2)}, u32[]{:S(2)}) collective-permute-start(f32[1,24,4,1]{1,2,3,0:T(4,128)S(1)} %get-tuple-element.10), channel_id=1, source_target_pairs={{1,0},{2,1},{3,2},{5,4},{6,5},{7,6},{9,8},{10,9},{11,10},{13,12},{... | collective-permute-start | bytes 1160 | tf_op jit(solution)/shard_map/ppermute | solution.py:17
  18.9 7.0 %collective-permute-start.6 = (f32[1,24,4,1]{1,2,3,0:T(4,128)S(1)}, f32[1,24,4,1]{1,2,3,0:T(4,128)S(1)}, u32[]{:S(2)}, u32[]{:S(2)}) collective-permute-start(f32[1,24,4,1]{1,2,3,0:T(4,128)S(1)} %get-tuple-element.9), channel_id=1, source_target_pairs={{0,1},{1,2},{2,3},{4,5},{5,6},{6,7},{8,9},{9,10},{10,11},{12,13},{... | collective-permute-start | bytes 1160 | tf_op jit(solution)/shard_map/ppermute | solution.py:16
  25.8 141.9 %all-reduce.6.cloned.1.call-start = ((), (), s32[]{:S(2)}) async-start(), calls=%async_computation.1 | async-start | bytes 262144
  50.3 6.2 %collective-permute-start = (f32[4,4,8,128]{3,2,1,0:T(8,128)S(1)}, f32[4,4,8,128]{3,2,1,0:T(8,128)S(1)}, u32[]{:S(2)}, u32[]{:S(2)}) collective-permute-start(f32[4,4,8,128]{3,2,1,0:T(8,128)S(1)} %get-tuple-element.8), channel_id=1, source_target_pairs={{0,4},{4,8},{8,12},{1,5},{5,9},{9,13},{2,6},{6,10},{10,14},{3,7},{... | collective-permute-start | bytes 196616 | tf_op jit(solution)/shard_map/ppermute | solution.py:16
  53.9 6.1 %collective-permute-start.1 = (f32[4,4,8,128]{3,2,1,0:T(8,128)S(1)}, f32[4,4,8,128]{3,2,1,0:T(8,128)S(1)}, u32[]{:S(2)}, u32[]{:S(2)}) collective-permute-start(f32[4,4,8,128]{3,2,1,0:T(8,128)S(1)} %get-tuple-element.7), channel_id=1, source_target_pairs={{4,0},{8,4},{12,8},{5,1},{9,5},{13,9},{6,2},{10,6},{14,10},{7,3},{... | collective-permute-start | bytes 196616 | tf_op jit(solution)/shard_map/ppermute | solution.py:17
  60.1 4.5 %collective-permute-start.3 = (f32[4,24,4,128]{3,2,1,0:T(4,128)S(1)}, f32[4,24,4,128]{3,2,1,0:T(4,128)S(1)}, u32[]{:S(2)}, u32[]{:S(2)}) collective-permute-start(f32[4,24,4,128]{3,2,1,0:T(4,128)S(1)} %get-tuple-element.6), channel_id=1, source_target_pairs={{1,0},{2,1},{3,2},{5,4},{6,5},{7,6},{9,8},{10,9},{11,10},{13,12},{... | collective-permute-start | bytes 589832 | tf_op jit(solution)/shard_map/ppermute | solution.py:17
  61.4 4.1 %collective-permute-start.2 = (f32[4,24,4,128]{3,2,1,0:T(4,128)S(1)}, f32[4,24,4,128]{3,2,1,0:T(4,128)S(1)}, u32[]{:S(2)}, u32[]{:S(2)}) collective-permute-start(f32[4,24,4,128]{3,2,1,0:T(4,128)S(1)} %get-tuple-element.5), channel_id=1, source_target_pairs={{0,1},{1,2},{2,3},{4,5},{5,6},{6,7},{8,9},{9,10},{10,11},{12,13},{... | collective-permute-start | bytes 589832 | tf_op jit(solution)/shard_map/ppermute | solution.py:16
  66.6 7.6 %copy-start.1 = (u32[32]{0:T(128)S(1)}, u32[32]{0:T(128)}, u32[]{:S(2)}) copy-start(u32[32]{0:T(128)} %constant.3) | copy-start | bytes 388
Sparse Core Ops, SparseCore 0:
  25.9 23.4 all-reduce.3
  74.3 93.3 all-reduce.5
where the time goes:
time: 176 us
  waiting for transfers between devices  119 us (68%)
  starting transfers between devices  20.4 us (12%)
  between operations  14.3 us (8%)
  local copies, waits for them, and re-layouts  11.7 us (7%)
  matrix products  9.06 us (5%)
    unnamed x3, waiting for transfers between devices  92.3 us
    psum x1, waiting for transfers between devices, per_device(): whole_sum = lax.psum(partials, 'sens')  23.3 us
    ppermute x4, starting transfers between devices, extended(): before = lax.ppermute(last, axis, up)  13.4 us
    ppermute x4, starting transfers between devices, extended(): after = lax.ppermute(first, axis, down)  6.92 us
    conv_general_dilated x1, matrix products, per_device(): lax.conv_general_dilated(flipped, kernel_rows, (1,), [(0, window - 1)], d...  6.13 us
  transfers between devices with their start and end apart: 10, of which 4 were waited for; matrix products, arithmetic and copies ran while one was open for 6% of the time, Pallas kernels for 0%

commit v1 on v0

--- a/solution.py
+++ b/solution.py
@@ -50,7 +50,7 @@
         preferred_element_type=jnp.float32,
     )
     partials = partials.reshape(vectors, cells_x, cells_y, window)
-    whole_sum = lax.psum(partials, "sens")
+    whole_sum = jnp.sum(lax.all_gather(partials, "sens"), axis=0)
     smoothed = smooth(whole_sum, diffusion).astype(jnp.bfloat16)
     flipped = smoothed.reshape(vectors, cells_x * cells_y, window)[:, :, ::-1]
     backward = lax.conv_general_dilated(

time: 176 us -> 161 us (0.915)
  waiting for transfers between devices: 119 us -> 100 us
  blocking collectives: 0 us -> 8.15 us
  local copies, waits for them, and re-layouts: 11.7 us -> 8.35 us
    psum x1 -> x0, waiting for transfers between devices: 23.3 us -> none  [per_device(): whole_sum = lax.psum(partials, 'sens')]
    all_gather x0 -> x1, blocking collectives: none -> 8.15 us  [per_device(): whole_sum = jnp.sum(lax.all_gather(partials, 'sens'), axis=0)]
    ppermute x4, waiting for transfers between devices: 2.68 us -> 7.82 us  [extended(): after = lax.ppermute(first, axis, down)]
    unnamed x10, local copies, waits for them, and re-layouts: 3.31 us -> 1.51 us
    ppermute x4, starting transfers between devices: 13.4 us -> 11.6 us  [extended(): before = lax.ppermute(last, axis, up)]
    unnamed x3 -> x2, waiting for transfers between devices: 92.3 us -> 92.7 us
  transfers between devices with their start and end apart: 10 -> 9, of which waited for: 4 -> 3; matrix products, arithmetic and copies ran while one was open for 6% -> 5% of each run, Pallas kernels for 0% -> 0%
where the time goes in v1:
time: 161 us; the launch traced here: 160 us
  waiting for transfers between devices  100 us (62%)
  starting transfers between devices  18.9 us (12%)
  between operations  14.3 us (9%)
  matrix products  9.06 us (6%)
  local copies, waits for them, and re-layouts  8.35 us (5%)
  blocking collectives  8.15 us (5%)
    unnamed x2, waiting for transfers between devices  92.7 us
    ppermute x4, starting transfers between devices, extended(): before = lax.ppermute(last, axis, up)  11.6 us
    all_gather x1, blocking collectives, per_device(): whole_sum = jnp.sum(lax.all_gather(partials, 'sens'), axis=0)  8.15 us
    ppermute x4, waiting for transfers between devices, extended(): after = lax.ppermute(first, axis, down)  7.82 us
    ppermute x4, starting transfers between devices, extended(): after = lax.ppermute(first, axis, down)  7.29 us
    conv_general_dilated x1, matrix products, per_device(): lax.conv_general_dilated(flipped, kernel_rows, (1,), [(0, window - 1)], d...  6.13 us
    reshape x1, local copies, waits for them, and re-layouts, per_device(): kernel_rows = kernel.reshape(kernel.shape[0], cells_x * cells_y, window)  3.33 us
  transfers between devices with their start and end apart: 9, of which 3 were waited for; matrix products, arithmetic and copies ran while one was open for 5% of the time, Pallas kernels for 0%

profile of v1, /device:TPU:8, one launch (start us, length us, event | category | flops | bytes accessed | tf_op | source)
XLA Modules:
  0.0 160.5 jit_solution(4046373324256067279)
XLA Ops:
  6.5 0.0 all-reduce.3.cloned.1.call-start
  6.5 0.8 fusion.17
  7.4 3.5 %collective-permute-start.4 = (f32[1,4,8,1]{1,2,3,0:T(8,128)S(1)}, f32[1,4,8,1]{1,2,3,0:T(8,128)S(1)}, u32[]{:S(2)}, u32[]{:S(2)}) collective-permute-start(f32[1,4,8,1]{1,2,3,0:T(8,128)S(1)} %get-tuple-element.11), channel_id=1, source_target_pairs={{0,4},{4,8},{8,12},{1,5},{5,9},{9,13},{2,6},{6,10},{10,14},{3,7},{... | collective-permute-start | bytes 392 | tf_op jit(solution)/shard_map/ppermute | solution.py:16
  10.9 2.4 %collective-permute-start.5 = (f32[1,4,8,1]{1,2,3,0:T(8,128)S(1)}, f32[1,4,8,1]{1,2,3,0:T(8,128)S(1)}, u32[]{:S(2)}, u32[]{:S(2)}) collective-permute-start(f32[1,4,8,1]{1,2,3,0:T(8,128)S(1)} %get-tuple-element.12), channel_id=1, source_target_pairs={{4,0},{8,4},{12,8},{5,1},{9,5},{13,9},{6,2},{10,6},{14,10},{7,3},{... | collective-permute-start | bytes 392 | tf_op jit(solution)/shard_map/ppermute | solution.py:17
  13.2 0.0 copy-start.1
  13.2 3.3 %copy.23 = bf16[64,128,128]{1,0,2:T(8,128)(2,1)S(1)} copy(bf16[64,128,128]{2,1,0:T(8,128)(2,1)} %bitcast.16) | data formatting | bytes 4194304 | tf_op jit(solution)/shard_map/reshape | solution.py:43
  16.6 0.0 copy-done.1
  16.6 0.1 copy.22
  16.7 0.0 copy-start
  16.7 2.9 %fusion.18 = f32[4,128,128]{1,0,2:T(4,128)S(1)} fusion(bf16[4,64,128]{1,0,2:T(4,128)(2,1)S(1)} %copy.22, bf16[64,128,128]{1,0,2:T(8,128)(2,1)S(1)} %copy.23), kind=kOutput, calls=%fused_computation.38 | convolution fusion | flops 541065216 | bytes 2424832 | tf_op jit(solution)/shard_map/conv_general_dilated | solution.py:44
  19.7 0.1 copy.24
  19.8 8.2 %all_gather.3 = f32[2,4,16,8,128]{4,3,2,1,0:T(8,128)S(1)} all-gather(f32[1,4,16,8,128]{4,3,2,1,0:T(8,128)S(1)} %bitcast.17), channel_id=1, replica_groups=mesh['sens'=2,'sx'=4,'sy'=4] {'sens'}, dimensions={0}, use_global_device_ids=true | all-gather | bytes 786432 | tf_op jit(solution)/shard_map/all_gather | solution.py:53
  28.0 0.0 collective-permute-done.4
  28.0 0.0 collective-permute-done.5
  28.0 0.0 copy-done
  28.0 0.1 pad_maximum_fusion.3
  28.1 1.3 collective-permute-start.6
  29.4 1.3 collective-permute-start.7
  30.7 3.5 %collective-permute-start = (f32[4,4,8,128]{3,2,1,0:T(8,128)S(1)}, f32[4,4,8,128]{3,2,1,0:T(8,128)S(1)}, u32[]{:S(2)}, u32[]{:S(2)}) collective-permute-start(f32[4,4,8,128]{3,2,1,0:T(8,128)S(1)} %get-tuple-element.7), channel_id=1, source_target_pairs={{0,4},{4,8},{8,12},{1,5},{5,9},{9,13},{2,6},{6,10},{10,14},{3,7},{... | collective-permute-start | bytes 196616 | tf_op jit(solution)/shard_map/ppermute | solution.py:16
  34.2 2.4 %collective-permute-start.1 = (f32[4,4,8,128]{3,2,1,0:T(8,128)S(1)}, f32[4,4,8,128]{3,2,1,0:T(8,128)S(1)}, u32[]{:S(2)}, u32[]{:S(2)}) collective-permute-start(f32[4,4,8,128]{3,2,1,0:T(8,128)S(1)} %get-tuple-element.8), channel_id=1, source_target_pairs={{4,0},{8,4},{12,8},{5,1},{9,5},{13,9},{6,2},{10,6},{14,10},{7,3},{... | collective-permute-start | bytes 196616 | tf_op jit(solution)/shard_map/ppermute | solution.py:17
  36.6 0.1 copy.28
  36.6 0.0 collective-permute-done.6
  36.6 0.0 collective-permute-done.7
  36.6 0.1 pad_maximum_fusion.2
  36.7 0.1 slice_bitcast_fusion.2
  36.8 0.1 slice_bitcast_fusion.1
  36.9 0.1 copy.25
  37.0 0.1 copy.26
  37.1 0.0 collective-permute-done
  37.1 3.3 %collective-permute-done.1 = f32[4,4,8,128]{3,2,1,0:T(8,128)S(1)} collective-permute-done((f32[4,4,8,128]{3,2,1,0:T(8,128)S(1)}, f32[4,4,8,128]{3,2,1,0:T(8,128)S(1)}, u32[]{:S(2)}, u32[]{:S(2)}) %collective-permute-start.1) | collective-permute-done | bytes 65568 | tf_op jit(solution)/shard_map/ppermute | solution.py:17
  40.4 0.1 fusion.14
  40.5 3.4 %collective-permute-start.2 = (f32[4,24,4,128]{3,2,1,0:T(4,128)S(1)}, f32[4,24,4,128]{3,2,1,0:T(4,128)S(1)}, u32[]{:S(2)}, u32[]{:S(2)}) collective-permute-start(f32[4,24,4,128]{3,2,1,0:T(4,128)S(1)} %get-tuple-element.5), channel_id=1, source_target_pairs={{0,1},{1,2},{2,3},{4,5},{5,6},{6,7},{8,9},{9,10},{10,11},{12,13},{... | collective-permute-start | bytes 589832 | tf_op jit(solution)/shard_map/ppermute | solution.py:16
  43.8 1.3 collective-permute-start.3
  45.1 0.1 slice_bitcast_fusion
  45.2 0.1 copy.27
  45.3 0.0 collective-permute-done.2
  45.3 4.5 %collective-permute-done.3 = f32[4,24,4,128]{3,2,1,0:T(4,128)S(1)} collective-permute-done((f32[4,24,4,128]{3,2,1,0:T(4,128)S(1)}, f32[4,24,4,128]{3,2,1,0:T(4,128)S(1)}, u32[]{:S(2)}, u32[]{:S(2)}) %collective-permute-start.3) | collective-permute-done | bytes 196640 | tf_op jit(solution)/shard_map/ppermute | solution.py:17
  49.8 0.1 pad_maximum_fusion
  50.0 0.3 fusion.2
  50.3 0.3 fusion.5
  50.5 0.2 fusion.8
  50.8 0.1 fusion.13
  50.9 0.0 copy-start.2
  50.9 0.4 rev.6
  51.3 0.1 copy.29
  51.5 6.1 %fusion.19 = f32[4,64,128]{1,0,2:T(4,128)S(1)} fusion(bf16[4,128,128]{1,0,2:T(4,128)(2,1)S(1)} %copy.29, bf16[64,128,128]{1,0,2:T(8,128)(2,1)S(1)} %copy.23), kind=kOutput, calls=%fused_computation.39 | convolution fusion | flops 541065216 | bytes 2359296 | tf_op jit(solution)/shard_map/conv_general_dilated | solution.py:56
  57.6 0.8 copy.31
  58.4 0.0 all-reduce.3.cloned.1.call-update
  58.4 0.0 copy-done.2
  58.5 0.6 dynamic-slice
  59.7 92.6 %all-reduce.3.cloned.1.call-done = f32[4,64,128]{2,0,1:T(4,128)} async-done(((f32[4,64,128]{2,0,1:T(4,128)}), f32[4,64,128]{2,0,1:T(4,128)}) %all-reduce.3.cloned.1.call-update) | async-done | bytes 131088
  152.3 0.7 constant_dynamic-slice_fusion
  153.0 0.6 copy.32
  (5 shorter events, 0.1 us)
Async XLA Ops:
  6.5 145.8 %all-reduce.3.cloned.1.call-start = ((), (), s32[]{:S(2)}) async-start(), calls=%async_computation | async-start | bytes 262144
  7.4 20.6 %collective-permute-start.4 = (f32[1,4,8,1]{1,2,3,0:T(8,128)S(1)}, f32[1,4,8,1]{1,2,3,0:T(8,128)S(1)}, u32[]{:S(2)}, u32[]{:S(2)}) collective-permute-start(f32[1,4,8,1]{1,2,3,0:T(8,128)S(1)} %get-tuple-element.11), channel_id=1, source_target_pairs={{0,4},{4,8},{8,12},{1,5},{5,9},{9,13},{2,6},{6,10},{10,14},{3,7},{... | collective-permute-start | bytes 392 | tf_op jit(solution)/shard_map/ppermute | solution.py:16
  10.9 17.2 %collective-permute-start.5 = (f32[1,4,8,1]{1,2,3,0:T(8,128)S(1)}, f32[1,4,8,1]{1,2,3,0:T(8,128)S(1)}, u32[]{:S(2)}, u32[]{:S(2)}) collective-permute-start(f32[1,4,8,1]{1,2,3,0:T(8,128)S(1)} %get-tuple-element.12), channel_id=1, source_target_pairs={{4,0},{8,4},{12,8},{5,1},{9,5},{13,9},{6,2},{10,6},{14,10},{7,3},{... | collective-permute-start | bytes 392 | tf_op jit(solution)/shard_map/ppermute | solution.py:17
  13.2 3.4 %copy-start.1 = (bf16[4,64,128]{2,1,0:T(8,128)(2,1)S(1)}, bf16[4,64,128]{2,1,0:T(8,128)(2,1)}, u32[]{:S(2)}) copy-start(bf16[4,64,128]{2,1,0:T(8,128)(2,1)} %param.3) | copy-start | bytes 196612
  16.7 11.3 %copy-start = (f32[16,8]{0,1:T(8,128)S(1)}, f32[16,8]{0,1:T(8,128)}, u32[]{:S(2)}) copy-start(f32[16,8]{0,1:T(8,128)} %param.5) | copy-start | bytes 1540
  28.1 8.5 %collective-permute-start.6 = (f32[1,24,4,1]{1,2,3,0:T(4,128)S(1)}, f32[1,24,4,1]{1,2,3,0:T(4,128)S(1)}, u32[]{:S(2)}, u32[]{:S(2)}) collective-permute-start(f32[1,24,4,1]{1,2,3,0:T(4,128)S(1)} %get-tuple-element.9), channel_id=1, source_target_pairs={{0,1},{1,2},{2,3},{4,5},{5,6},{6,7},{8,9},{9,10},{10,11},{12,13},{... | collective-permute-start | bytes 1160 | tf_op jit(solution)/shard_map/ppermute | solution.py:16
  29.4 7.3 %collective-permute-start.7 = (f32[1,24,4,1]{1,2,3,0:T(4,128)S(1)}, f32[1,24,4,1]{1,2,3,0:T(4,128)S(1)}, u32[]{:S(2)}, u32[]{:S(2)}) collective-permute-start(f32[1,24,4,1]{1,2,3,0:T(4,128)S(1)} %get-tuple-element.10), channel_id=1, source_target_pairs={{1,0},{2,1},{3,2},{5,4},{6,5},{7,6},{9,8},{10,9},{11,10},{13,12},{... | collective-permute-start | bytes 1160 | tf_op jit(solution)/shard_map/ppermute | solution.py:17
  30.7 6.4 %collective-permute-start = (f32[4,4,8,128]{3,2,1,0:T(8,128)S(1)}, f32[4,4,8,128]{3,2,1,0:T(8,128)S(1)}, u32[]{:S(2)}, u32[]{:S(2)}) collective-permute-start(f32[4,4,8,128]{3,2,1,0:T(8,128)S(1)} %get-tuple-element.7), channel_id=1, source_target_pairs={{0,4},{4,8},{8,12},{1,5},{5,9},{9,13},{2,6},{6,10},{10,14},{3,7},{... | collective-permute-start | bytes 196616 | tf_op jit(solution)/shard_map/ppermute | solution.py:16
  34.2 6.2 %collective-permute-start.1 = (f32[4,4,8,128]{3,2,1,0:T(8,128)S(1)}, f32[4,4,8,128]{3,2,1,0:T(8,128)S(1)}, u32[]{:S(2)}, u32[]{:S(2)}) collective-permute-start(f32[4,4,8,128]{3,2,1,0:T(8,128)S(1)} %get-tuple-element.8), channel_id=1, source_target_pairs={{4,0},{8,4},{12,8},{5,1},{9,5},{13,9},{6,2},{10,6},{14,10},{7,3},{... | collective-permute-start | bytes 196616 | tf_op jit(solution)/shard_map/ppermute | solution.py:17
  40.5 4.8 %collective-permute-start.2 = (f32[4,24,4,128]{3,2,1,0:T(4,128)S(1)}, f32[4,24,4,128]{3,2,1,0:T(4,128)S(1)}, u32[]{:S(2)}, u32[]{:S(2)}) collective-permute-start(f32[4,24,4,128]{3,2,1,0:T(4,128)S(1)} %get-tuple-element.5), channel_id=1, source_target_pairs={{0,1},{1,2},{2,3},{4,5},{5,6},{6,7},{8,9},{9,10},{10,11},{12,13},{... | collective-permute-start | bytes 589832 | tf_op jit(solution)/shard_map/ppermute | solution.py:16
  43.8 6.0 %collective-permute-start.3 = (f32[4,24,4,128]{3,2,1,0:T(4,128)S(1)}, f32[4,24,4,128]{3,2,1,0:T(4,128)S(1)}, u32[]{:S(2)}, u32[]{:S(2)}) collective-permute-start(f32[4,24,4,128]{3,2,1,0:T(4,128)S(1)} %get-tuple-element.6), channel_id=1, source_target_pairs={{1,0},{2,1},{3,2},{5,4},{6,5},{7,6},{9,8},{10,9},{11,10},{13,12},{... | collective-permute-start | bytes 589832 | tf_op jit(solution)/shard_map/ppermute | solution.py:17
  50.9 7.6 %copy-start.2 = (u32[32]{0:T(128)S(1)}, u32[32]{0:T(128)}, u32[]{:S(2)}) copy-start(u32[32]{0:T(128)} %constant.4) | copy-start | bytes 388
Sparse Core Ops, SparseCore 0:
  58.6 93.7 all-reduce.2
